TPU v7x, 32 devices: a whole 2x2x4 slice. The times are simulated.
32 devices in a mesh: batch: 8 (over y, x, core), head: 4 (over z).
Axes of the slice: x: 2, y: 2, z: 4, core: 2. Of those that a mesh axis runs over, the one named last changes fastest.
Arguments:
- layer_input: bfloat16 [16384, 768], P(('batch', 'head')), may hold values from -6 to 6
- memory_flags: int32 [32], P('batch'), may hold values 0 or 1
- document_start: int32 [32], P('batch'), may hold values from 1 to 511
- memory_coefficients: bfloat16 [32, 256, 768], P('batch'), may hold values from -6 to 6
- first_gain: bfloat16 [768], replicated, may hold values from 0.5 to 1.5
- first_shift: bfloat16 [768], replicated, may hold values from -1 to 1
- query_weight: bfloat16 [768, 768], P(None, 'head'), may hold values from -0.3125 to 0.3125
- query_bias: bfloat16 [768], P('head'), may hold values from -1 to 1
- key_matrix: bfloat16 [768, 768], P(None, 'head'), may hold values from -0.21875 to 0.21875
- value_matrix: bfloat16 [768, 768], P(None, 'head'), may hold values from -0.21875 to 0.21875
- value_offset_bias: bfloat16 [768], P('head'), may hold values from -1 to 1
- out_weight: bfloat16 [768, 768], P('head'), may hold values from -0.875 to 0.875
- out_bias: bfloat16 [768], replicated, may hold values from -1 to 1
- second_gain: bfloat16 [768], replicated, may hold values from 0.5 to 1.5
- second_shift: bfloat16 [768], replicated, may hold values from -1 to 1
- up_weight: bfloat16 [768, 3072], P(None, 'head'), may hold values from -0.21875 to 0.21875
- up_bias: bfloat16 [3072], P('head'), may hold values from -1 to 1
- down_weight: bfloat16 [3072, 768], P('head'), may hold values from -0.109375 to 0.109375
- down_bias: bfloat16 [768], replicated, may hold values from -1 to 1
- centre_weight: float32 [12, 256], P('head'), may hold values from -0.375 to 0.375
- width_weight: float32 [12, 256], P('head'), may hold values from -0.375 to 0.375
- grad_output: bfloat16 [16384, 768], P(('batch', 'head')), may hold values from -6 to 6
Outputs:
- layer_output: bfloat16 [16384, 768], P(('batch', 'head'))
- input_grad: bfloat16 [16384, 768], P(('batch', 'head'))
- first_gain_grad: float32 [768], replicated
- first_shift_grad: float32 [768], replicated
- query_weight_grad: float32 [768, 768], P(None, 'head')
- query_bias_grad: float32 [768], P('head')
- key_weight_grad: float32 [768, 768], P(None, 'head')
- value_weight_grad: float32 [768, 768], P(None, 'head')
- value_bias_grad: float32 [768], P('head')
- out_weight_grad: float32 [768, 768], P('head')
- out_bias_grad: float32 [768], replicated
- second_gain_grad: float32 [768], replicated
- second_shift_grad: float32 [768], replicated
- up_weight_grad: float32 [768, 3072], P(None, 'head')
- up_bias_grad: float32 [3072], P('head')
- down_weight_grad: float32 [3072, 768], P('head')
- down_bias_grad: float32 [768], replicated
- centre_weight_grad: float32 [12, 256], P('head')
- width_weight_grad: float32 [12, 256], P('head')
Inputs may be any that keep to these rules, and one draw needn't show every extreme that they name: `memory_flags`: 1 marks a segment with memory.
All inputs are finite; a program needn't handle non-finite values. No bound on the sum of `memory_flags` on one device may be relied on, other than what follows from the above.
Results may differ from a plain program's by a relative error of at most 0.018.
The roundings to bfloat16 on the way count: a program that leaves them out, or rounds other values in their place, can miss the bound.
Values may be sent and summed in bfloat16 or wider, within the bound.
A program may use at most 128 MiB of HBM per device.

v0:
```python
import math
import jax
import jax.numpy as jnp
from jax import lax
from jax.sharding import PartitionSpec as P


def norm_stats(values_in):
    center = values_in - jnp.mean(values_in, axis=-1, keepdims=True)
    factor = lax.rsqrt(jnp.mean(center * center, axis=-1, keepdims=True) + 1e-05)
    return (center * factor, factor)


def norm_back(grad, normed, factor):
    return factor * (
        grad
        - jnp.mean(grad, axis=-1, keepdims=True)
        - normed * jnp.mean(grad * normed, axis=-1, keepdims=True)
    )


def cross_dot(left, right):
    return lax.dot_general(
        left, right, (((0,), (0,)), ((), ())), preferred_element_type=jnp.float32
    )


def back_dot(left, right):
    return lax.dot_general(
        left, right, (((1,), (1,)), ((), ())), preferred_element_type=jnp.float32
    )


def segment_mask(length, bound):
    row_ids = lax.broadcasted_iota(jnp.int32, (length, length), 0)
    col_ids = lax.broadcasted_iota(jnp.int32, (length, length), 1)
    return (col_ids <= row_ids) & ((col_ids >= bound) | (row_ids < bound))


def masked_scores(queries, keys_low, bound):
    factor = queries.shape[-1] ** (-0.5)
    scores = (
        jnp.einsum("qhd,khd->hqk", queries, keys_low, preferred_element_type=jnp.float32) * factor
    )
    return jnp.where(segment_mask(queries.shape[0], bound)[None], scores, -1000000000.0)


def recall_terms(queries, memory_keys, centre_weight, width_weight):
    factor = queries.shape[-1] ** (-0.5)
    mem_scores = (
        jnp.einsum("qhd,nhd->hqn", queries, memory_keys, preferred_element_type=jnp.float32)
        * factor
    )
    centre = jax.nn.sigmoid(
        jnp.einsum("hqn,hn->hq", mem_scores, centre_weight, precision=lax.Precision.HIGHEST)
    )
    width_pre = jnp.einsum("hqn,hn->hq", mem_scores, width_weight, precision=lax.Precision.HIGHEST)
    spread = 0.02 * jax.nn.softplus(width_pre) + 0.01
    basis_count = memory_keys.shape[0]
    centres = (jnp.arange(basis_count, dtype=jnp.float32) + 0.5) / basis_count
    offset = centre[..., None] - centres
    recall = (
        jnp.exp(-offset * offset / (2.0 * spread[..., None]))
        * lax.rsqrt(2.0 * math.pi * spread[..., None])
        / basis_count
    )
    return (mem_scores, centre, width_pre, spread, offset, recall)


def forward_segment(segment_item, centre_weight, width_weight):
    queries, keys_low, values, memory_keys, memory_values, flag, bound = segment_item
    scores = masked_scores(queries, keys_low, bound)
    row_peak = jnp.max(scores, axis=-1, keepdims=True)
    shifted = jnp.exp(scores - row_peak)
    row_total = jnp.sum(shifted, axis=-1, keepdims=True)
    probs_low = (shifted / row_total).astype(jnp.bfloat16)
    local_mix = jnp.einsum("hqk,khd->qhd", probs_low, values, preferred_element_type=jnp.float32)
    recall_low = recall_terms(queries, memory_keys, centre_weight, width_weight)[5].astype(
        jnp.bfloat16
    )
    recalled = jnp.einsum(
        "hqn,nhd->qhd", recall_low, memory_values, preferred_element_type=jnp.float32
    )
    context = (local_mix + flag * recalled).astype(jnp.bfloat16)
    return (context, (row_peak + jnp.log(row_total))[..., 0])


def backward_segment(segment_item, centre_weight, width_weight):
    queries, keys_low, values, memory_keys, memory_values, flag, bound, log_total, grad_context = (
        segment_item
    )
    factor = queries.shape[-1] ** (-0.5)
    scores = masked_scores(queries, keys_low, bound)
    attn_probs = jnp.exp(scores - log_total[..., None])
    probs_low = attn_probs.astype(jnp.bfloat16)
    grad_values = jnp.einsum(
        "hqk,qhd->khd", probs_low, grad_context, preferred_element_type=jnp.float32
    )
    grad_probs = jnp.einsum(
        "qhd,khd->hqk", grad_context, values, preferred_element_type=jnp.float32
    )
    grad_scores = (
        attn_probs * (grad_probs - jnp.sum(attn_probs * grad_probs, axis=-1, keepdims=True))
    ).astype(jnp.bfloat16)
    mem_scores, centre, width_pre, spread, offset, recall = recall_terms(
        queries, memory_keys, centre_weight, width_weight
    )
    recall_low = recall.astype(jnp.bfloat16)
    grad_recall = flag * jnp.einsum(
        "qhd,nhd->hqn", grad_context, memory_values, preferred_element_type=jnp.float32
    )
    memory_value_gradient = flag * jnp.einsum(
        "hqn,qhd->nhd", recall_low, grad_context, preferred_element_type=jnp.float32
    )
    weighted = grad_recall * recall
    spread_b = spread[..., None]
    grad_centre = jnp.sum(weighted * (-offset / spread_b), axis=-1)
    grad_spread = jnp.sum(
        weighted * (offset * offset / (2.0 * spread_b * spread_b) - 0.5 / spread_b), axis=-1
    )
    centre_pre_grad = grad_centre * centre * (1.0 - centre)
    width_pre_grad = grad_spread * 0.02 * jax.nn.sigmoid(width_pre)
    grad_mem_scores = (
        centre_pre_grad[..., None] * centre_weight[:, None, :]
        + width_pre_grad[..., None] * width_weight[:, None, :]
    ).astype(jnp.bfloat16)
    centre_grad = jnp.einsum(
        "hq,hqn->hn", centre_pre_grad, mem_scores, precision=lax.Precision.HIGHEST
    )
    width_grad = jnp.einsum(
        "hq,hqn->hn", width_pre_grad, mem_scores, precision=lax.Precision.HIGHEST
    )
    grad_queries = factor * (
        jnp.einsum("hqk,khd->qhd", grad_scores, keys_low, preferred_element_type=jnp.float32)
        + jnp.einsum(
            "hqn,nhd->qhd", grad_mem_scores, memory_keys, preferred_element_type=jnp.float32
        )
    )
    grad_keys = factor * jnp.einsum(
        "hqk,qhd->khd", grad_scores, queries, preferred_element_type=jnp.float32
    )
    memory_key_gradient = factor * jnp.einsum(
        "hqn,qhd->nhd", grad_mem_scores, queries, preferred_element_type=jnp.float32
    )
    return (
        grad_queries.astype(jnp.bfloat16),
        grad_keys.astype(jnp.bfloat16),
        grad_values.astype(jnp.bfloat16),
        memory_key_gradient.astype(jnp.bfloat16),
        memory_value_gradient.astype(jnp.bfloat16),
        centre_grad,
        width_grad,
    )


def per_device(
    layer_input,
    memory_flags,
    document_start,
    memory_coefficients,
    first_gain,
    first_shift,
    query_weight,
    query_bias,
    key_matrix,
    value_matrix,
    value_offset_bias,
    out_weight,
    out_bias,
    second_gain,
    second_shift,
    up_weight,
    up_bias,
    down_weight,
    down_bias,
    centre_weight,
    width_weight,
    grad_output,
):
    segments = memory_coefficients.shape[0]
    basis_count = memory_coefficients.shape[1]
    group_heads = centre_weight.shape[0]
    group_cols = query_weight.shape[1]
    head_size = group_cols // group_heads
    flag_values = memory_flags.astype(jnp.float32)
    inputs = layer_input.astype(jnp.float32)
    normed_one, factor_one = norm_stats(inputs)
    first_low = (normed_one * first_gain + first_shift).astype(jnp.bfloat16)
    first_rows = lax.all_gather(first_low, "head", axis=0, tiled=True)
    total_rows = first_rows.shape[0]
    length = total_rows // segments
    queries = (
        jnp.dot(first_rows, query_weight, preferred_element_type=jnp.float32) + query_bias
    ).astype(jnp.bfloat16)
    keys_low = jnp.dot(first_rows, key_matrix, preferred_element_type=jnp.float32).astype(
        jnp.bfloat16
    )
    values = (
        jnp.dot(first_rows, value_matrix, preferred_element_type=jnp.float32) + value_offset_bias
    ).astype(jnp.bfloat16)
    memory_keys = jnp.einsum(
        "wmr,rq->wmq", memory_coefficients, key_matrix, preferred_element_type=jnp.float32
    ).astype(jnp.bfloat16)
    memory_values = (
        jnp.einsum(
            "wmr,rq->wmq", memory_coefficients, value_matrix, preferred_element_type=jnp.float32
        )
        + value_offset_bias
    ).astype(jnp.bfloat16)
    tile_shape = (segments, length, group_heads, head_size)
    basis_dimensions = (segments, basis_count, group_heads, head_size)
    seg_items = (
        queries.reshape(tile_shape),
        keys_low.reshape(tile_shape),
        values.reshape(tile_shape),
        memory_keys.reshape(basis_dimensions),
        memory_values.reshape(basis_dimensions),
        flag_values,
        document_start,
    )
    context, log_total = lax.map(
        lambda segment_item: forward_segment(segment_item, centre_weight, width_weight), seg_items
    )
    context = context.reshape(total_rows, group_cols)
    attn_sum = lax.psum_scatter(
        jnp.dot(context, out_weight, preferred_element_type=jnp.float32).astype(jnp.bfloat16),
        "head",
        scatter_dimension=0,
        tiled=True,
    ).astype(jnp.float32)
    hidden = inputs + (attn_sum + out_bias)
    normed_two, factor_two = norm_stats(hidden)
    second_low = (normed_two * second_gain + second_shift).astype(jnp.bfloat16)
    second_rows = lax.all_gather(second_low, "head", axis=0, tiled=True)
    up_pre = jnp.dot(second_rows, up_weight, preferred_element_type=jnp.float32) + up_bias
    up_act = jax.nn.gelu(up_pre, approximate=True).astype(jnp.bfloat16)
    mlp_sum = lax.psum_scatter(
        jnp.dot(up_act, down_weight, preferred_element_type=jnp.float32).astype(jnp.bfloat16),
        "head",
        scatter_dimension=0,
        tiled=True,
    ).astype(jnp.float32)
    layer_output = (hidden + (mlp_sum + down_bias)).astype(jnp.bfloat16)
    down_bias_grad = jnp.sum(grad_output.astype(jnp.float32), axis=0)
    grad_rows = lax.all_gather(grad_output, "head", axis=0, tiled=True)
    down_weight_grad = cross_dot(up_act, grad_rows)
    grad_act = back_dot(grad_rows, down_weight)
    gelu_pull = jax.vjp(lambda values_in: jax.nn.gelu(values_in, approximate=True), up_pre)[1]
    grad_up = gelu_pull(grad_act)[0].astype(jnp.bfloat16)
    up_bias_grad = jnp.sum(grad_up.astype(jnp.float32), axis=0)
    up_weight_grad = cross_dot(second_rows, grad_up)
    grad_second = lax.psum_scatter(
        back_dot(grad_up, up_weight).astype(jnp.bfloat16), "head", scatter_dimension=0, tiled=True
    ).astype(jnp.float32)
    second_gain_grad = jnp.sum(grad_second * normed_two, axis=0)
    second_shift_grad = jnp.sum(grad_second, axis=0)
    grad_hidden = grad_output.astype(jnp.float32) + norm_back(
        grad_second * second_gain, normed_two, factor_two
    )
    branch_low = grad_hidden.astype(jnp.bfloat16)
    out_bias_grad = jnp.sum(branch_low.astype(jnp.float32), axis=0)
    branch_rows = lax.all_gather(branch_low, "head", axis=0, tiled=True)
    out_weight_grad = cross_dot(context, branch_rows)
    grad_context = back_dot(branch_rows, out_weight).astype(jnp.bfloat16)
    back_items = seg_items + (log_total, grad_context.reshape(tile_shape))
    results = lax.map(
        lambda segment_item: backward_segment(segment_item, centre_weight, width_weight), back_items
    )
    grad_queries = results[0].reshape(total_rows, group_cols)
    grad_keys = results[1].reshape(total_rows, group_cols)
    grad_values = results[2].reshape(total_rows, group_cols)
    memory_key_gradient = results[3].reshape(segments, basis_count, group_cols)
    memory_value_gradient = results[4].reshape(segments, basis_count, group_cols)
    centre_weight_grad = jnp.sum(results[5], axis=0)
    width_weight_grad = jnp.sum(results[6], axis=0)
    query_weight_grad = cross_dot(first_rows, grad_queries)
    query_bias_grad = jnp.sum(grad_queries.astype(jnp.float32), axis=0)
    key_weight_grad = cross_dot(first_rows, grad_keys) + jnp.einsum(
        "qwo,qwy->oy", memory_coefficients, memory_key_gradient, preferred_element_type=jnp.float32
    )
    value_weight_grad = cross_dot(first_rows, grad_values) + jnp.einsum(
        "qwo,qwy->oy",
        memory_coefficients,
        memory_value_gradient,
        preferred_element_type=jnp.float32,
    )
    value_bias_grad = jnp.sum(grad_values.astype(jnp.float32), axis=0) + jnp.sum(
        memory_value_gradient.astype(jnp.float32), axis=(0, 1)
    )
    grad_first = lax.psum_scatter(
        (
            back_dot(grad_queries, query_weight)
            + back_dot(grad_keys, key_matrix)
            + back_dot(grad_values, value_matrix)
        ).astype(jnp.bfloat16),
        "head",
        scatter_dimension=0,
        tiled=True,
    ).astype(jnp.float32)
    first_gain_grad = jnp.sum(grad_first * normed_one, axis=0)
    first_shift_grad = jnp.sum(grad_first, axis=0)
    input_grad = (grad_hidden + norm_back(grad_first * first_gain, normed_one, factor_one)).astype(
        jnp.bfloat16
    )
    (
        query_weight_grad,
        query_bias_grad,
        key_weight_grad,
        value_weight_grad,
        value_bias_grad,
        out_weight_grad,
        centre_weight_grad,
        width_weight_grad,
        down_weight_grad,
        up_weight_grad,
        up_bias_grad,
    ) = lax.psum(
        (
            query_weight_grad,
            query_bias_grad,
            key_weight_grad,
            value_weight_grad,
            value_bias_grad,
            out_weight_grad,
            centre_weight_grad,
            width_weight_grad,
            down_weight_grad,
            up_weight_grad,
            up_bias_grad,
        ),
        "batch",
    )
    (
        first_gain_grad,
        first_shift_grad,
        out_bias_grad,
        second_gain_grad,
        second_shift_grad,
        down_bias_grad,
    ) = lax.psum(
        (
            first_gain_grad,
            first_shift_grad,
            out_bias_grad,
            second_gain_grad,
            second_shift_grad,
            down_bias_grad,
        ),
        ("batch", "head"),
    )
    return (
        layer_output,
        input_grad,
        first_gain_grad,
        first_shift_grad,
        query_weight_grad,
        query_bias_grad,
        key_weight_grad,
        value_weight_grad,
        value_bias_grad,
        out_weight_grad,
        out_bias_grad,
        second_gain_grad,
        second_shift_grad,
        up_weight_grad,
        up_bias_grad,
        down_weight_grad,
        down_bias_grad,
        centre_weight_grad,
        width_weight_grad,
    )


def solution(mesh):
    placed = (
        P(("batch", "head"), None),
        P("batch"),
        P("batch"),
        P("batch", None, None),
        P(),
        P(),
        P(None, "head"),
        P("head"),
        P(None, "head"),
        P(None, "head"),
        P("head"),
        P("head", None),
        P(),
        P(),
        P(),
        P(None, "head"),
        P("head"),
        P("head", None),
        P(),
        P("head", None),
        P("head", None),
        P(("batch", "head"), None),
    )
    return jax.shard_map(
        per_device,
        mesh=mesh,
        in_specs=placed,
        out_specs=(
            P(("batch", "head"), None),
            P(("batch", "head"), None),
            P(),
            P(),
            P(None, "head"),
            P("head"),
            P(None, "head"),
            P(None, "head"),
            P("head"),
            P("head", None),
            P(),
            P(),
            P(),
            P(None, "head"),
            P("head"),
            P("head", None),
            P(),
            P("head", None),
            P("head", None),
        ),
        check_vma=False,
    )
```

profile of v0, /device:TPU:0, one launch (start us, length us, event | category | flops | bytes accessed | tf_op | source)
XLA Modules:
  0.0 868.7 jit_solution(15008076573527793442)
XLA Ops:
  14.6 64.0 %all-gather.5.cloned.1.call-done = bf16[2048,768]{1,0:T(8,128)(2,1)} async-done(((bf16[512,768]{1,0:T(8,128)(2,1)}), bf16[2048,768]{1,0:T(8,128)(2,1)}) %all-gather.5.cloned.1.call-update) | async-done | bytes 3145744 | tf_op jit(solution)/shard_map/all_gather | solution.py:189
  78.6 3.1 fusion.166
  84.5 3.9 fusion.165
  88.4 3.1 reshape.257
  91.6 2.2 copy.58
  93.7 4.0 convolution_convert_fusion.4
  97.7 3.0 reshape.259
  100.7 2.2 copy.60
  103.9 54.4 %while.34 = (s32[]{:T(128)}, bf16[4,512,3,64]{1,3,2,0:T(8,128)(2,1)}, f32[4,3,512]{2,1,0:T(4,128)}, bf16[4,512,3,64]{1,3,2,0:T(8,128)(2,1)}, s32[4]{0:T(128)S(1)...) while((s32[]{:T(128)}, ...), condition=%wide.region_5.6_spmd, body=%wide.region_2.5_spmd.sunk | while | flops 325111296 | bytes 17297064 | solution.py:221
  111.6 2.0 fusion.318
  114.3 3.2 fusion.321
  125.2 2.0 fusion.318
  127.9 3.2 fusion.321
  138.8 2.0 fusion.318
  141.5 3.2 fusion.321
  152.4 2.0 fusion.318
  155.0 3.2 fusion.321
  161.1 2.7 convolution_convert_fusion.2
  166.4 56.4 %reduce-scatter.5.cloned.1.call-done = bf16[512,768]{1,0:T(8,128)(2,1)} async-done(((bf16[2048,768]{1,0:T(8,128)(2,1)}), bf16[512,768]{1,0:T(8,128)(2,1)}) %reduce-scatter.5.cloned.1.call-update) | async-done | bytes 786448 | tf_op jit(solution)/shard_map/reduce_scatter | solution.py:225
  228.9 61.8 %all-gather.7.cloned.1.call-done = bf16[2048,768]{1,0:T(8,128)(2,1)} async-done(((bf16[512,768]{1,0:T(8,128)(2,1)}), bf16[2048,768]{1,0:T(8,128)(2,1)}) %all-gather.7.cloned.1.call-update) | async-done | bytes 3145744 | tf_op jit(solution)/shard_map/all_gather | solution.py:234
  290.6 7.5 fusion.196
  298.1 56.1 %all-gather.9.cloned.1.call-done = bf16[2048,768]{1,0:T(8,128)(2,1)} async-done(((bf16[512,768]{1,0:T(8,128)(2,1)}), bf16[2048,768]{1,0:T(8,128)(2,1)}) %all-gather.9.cloned.1.call-update) | async-done | bytes 3145744 | tf_op jit(solution)/shard_map/all_gather | solution.py:245
  354.3 11.0 %convert_reduce_fusion = (f32[768]{0:T(1024)}, bf16[2048,768]{1,0:T(8,128)(2,1)S(1)}, bf16[2048,768]{1,0:T(8,128)(2,1)}) fusion(f32[2048,768]{1,0:T(8,128)} %fusion.196, f32[768]{0:T(1024)} %convert_element_type.193, bf16[2048,768]{1,0:T(8,128)(2,1)} %all-gather.9.cloned.1.call-done, bf16[768,768]{1,0:T(8,128)(2,1)} %param.43), kind=kOutput, calls=%fused_computation.206 | convolution fusion | flops 2455239936 | bytes 16914432 | tf_op jit(solution)/shard_map/dot_general | solution.py:29
  366.9 4.0 convolution_convert_fusion
  371.0 6.5 convolution_convert_fusion.1
  378.8 51.2 %reduce-scatter.9.cloned.1.call-done = bf16[512,768]{1,0:T(8,128)(2,1)} async-done(((bf16[2048,768]{1,0:T(8,128)(2,1)}), bf16[512,768]{1,0:T(8,128)(2,1)}) %reduce-scatter.9.cloned.1.call-update) | async-done | bytes 786448 | tf_op jit(solution)/shard_map/reduce_scatter | solution.py:252
  430.0 2.9 fusion.188
  433.5 59.0 %reduce-scatter.7.cloned.1.call-done = bf16[512,768]{1,0:T(8,128)(2,1)} async-done(((bf16[2048,768]{1,0:T(8,128)(2,1)}), bf16[512,768]{1,0:T(8,128)(2,1)}) %reduce-scatter.7.cloned.1.call-update) | async-done | bytes 786448 | tf_op jit(solution)/shard_map/reduce_scatter | solution.py:237
  492.5 5.3 convert_reduce_fusion.5
  497.8 63.6 %all-gather.11.cloned.1.call-done = bf16[2048,768]{1,0:T(8,128)(2,1)} async-done(((bf16[512,768]{1,0:T(8,128)(2,1)}), bf16[2048,768]{1,0:T(8,128)(2,1)}) %all-gather.11.cloned.1.call-update) | async-done | bytes 3145744 | tf_op jit(solution)/shard_map/all_gather | solution.py:262
  561.4 4.0 convolution_convert_fusion.3
  565.4 3.4 reshape.263
  568.8 2.2 copy.64
  573.9 91.2 %while.35 = (s32[]{:T(128)}, bf16[4,512,3,64]{1,3,2,0:T(8,128)(2,1)}, bf16[4,512,3,64]{1,3,2,0:T(8,128)(2,1)}, bf16[4,512,3,64]{1,3,2,0:T(8,128)(2,1)}, bf16[4,2...) while((s32[]{:T(128)}, ...), condition=%wide.region_17.18_spmd, body=%wide.region_13.17_spmd.sunk | while | flops 795121152 | bytes 42630428 | solution.py:266
  580.1 2.7 fusion.348
  602.8 2.7 fusion.348
  625.6 2.7 fusion.348
  648.4 2.7 fusion.348
  671.7 2.8 add_convert_fusion.3
  674.6 7.1 fusion.201
  681.7 4.2 fusion.200
  701.8 25.6 %all-reduce.1 = (f32[192]{0:T(256)}, f32[192]{0:T(256)}, f32[768]{0:T(1024)}, f32[3,256]{1,0:T(4,128)}, f32[3,256]{1,0:T(4,128)}) all-reduce(f32[192]{0:T(256)} %reduce_sum.229, f32[192]{0:T(256)S(1)} %add.258, f32[768]{0:T(1024)} %get-tuple-element.347, f32[3,256]{1,0:T(4,128)} %reduce_sum.237, ...), channel_id=1, replica_groups=mesh['batch'=8,'head'=4] {'batch'}, use_global_device_ids=true, to_apply=%region_27.28 | all-reduce | flops 2688 | bytes 21504 | tf_op jit(solution)/shard_map/psum | solution.py:317
  727.4 6.2 reduce-scatter.11.cloned.1.call-done
  733.6 2.0 fusion.189
  735.7 41.8 %all-reduce = (f32[768]{0:T(1024)}, f32[768]{0:T(1024)}, f32[768]{0:T(1024)}, f32[768]{0:T(1024)}, f32[768]{0:T(1024)}, /*index=5*/f32[768]{0:T(1024)}) all-reduce(f32[768]{0:T(1024)S(1)} %get-tuple-element.260, f32[768]{0:T(1024)S(1)} %get-tuple-element.265, ...), channel_id=1, replica_groups=mesh['batch'=8,'head'=4] {'batch','head'}, use_global_device_ids=true, to_apply=%region_22.23 | all-reduce | flops 4608 | bytes 36864 | tf_op jit(solution)/shard_map/psum | solution.py:340
  777.5 2.9 fusion.182
  780.4 73.2 %all-reduce.5.cloned.1.call-done = (f32[768,192]{0,1:T(8,128)}, f32[768,192]{0,1:T(8,128)}, f32[768,192]{0,1:T(8,128)}, f32[192,768]{1,0:T(8,128)}, f32[768,768]{1,0:T(8,128)}, /*index=5*/f32[768,768]{1,0:T(8,128)}) async-done(((f32[768,192]{0,1:T(8,128)}, f32[768,192]{0,1:T(8,128)}, f32[768,192]{0,1:T(8,128)}, f32[192,768]{1,0:T(8,128)}, f32[768,768]{1,0:T(8,128)}, /*index=5*/f32[768,768]{1,0:T(8,128)}), ...) | async-done | bytes 7077904 | tf_op jit(solution)/shard_map/psum | solution.py:317
  853.5 2.0 copy.222
  (365 shorter events, 170.6 us)
Async XLA Ops:
  7.2 5.2 copy-start
  7.2 3.8 copy-start.1
  7.2 3.1 copy-start.45
  7.2 3.2 copy-start.46
  7.2 71.4 %all-gather.5.cloned.1.call-start = ((), (), s32[]{:S(2)}) async-start(), calls=%async_computation.4 | async-start | bytes 3932160 | tf_op jit(solution)/shard_map/all_gather | solution.py:189
  8.8 3.6 copy-start.50
  8.8 3.6 copy-start.51
  8.8 3.6 copy-start.52
  8.8 3.6 copy-start.26
  12.3 210.6 %reduce-scatter.5.cloned.1.call-start = ((), (), s32[]{:S(2)}) async-start(), calls=%async_computation.5 | async-start | bytes 3932160 | tf_op jit(solution)/shard_map/reduce_scatter | solution.py:225
  100.7 3.2 copy-start.33
  100.7 3.2 copy-start.34
  100.7 3.2 copy-start.53
  158.3 2.9 copy-start.29
  163.8 126.8 %all-gather.7.cloned.1.call-start = ((), (), s32[]{:S(2)}) async-start(), calls=%async_computation.6 | async-start | bytes 3932160 | tf_op jit(solution)/shard_map/all_gather | solution.py:234
  222.9 2.7 copy-start.43
  227.0 127.3 %all-gather.9.cloned.1.call-start = ((), (), s32[]{:S(2)}) async-start(), calls=%async_computation.8 | async-start | bytes 3932160 | tf_op jit(solution)/shard_map/all_gather | solution.py:245
  227.6 202.4 %reduce-scatter.9.cloned.1.call-start = ((), (), s32[]{:S(2)}) async-start(), calls=%async_computation.9 | async-start | bytes 3932160 | tf_op jit(solution)/shard_map/reduce_scatter | solution.py:252
  354.3 12.6 %copy-start.49 = (bf16[768,768]{1,0:T(8,128)(2,1)S(1)}, bf16[768,768]{1,0:T(8,128)(2,1)}, u32[]{:S(2)}) copy-start(bf16[768,768]{1,0:T(8,128)(2,1)} %param.41) | copy-start | bytes 3538948
  370.9 121.5 %reduce-scatter.7.cloned.1.call-start = ((), (), s32[]{:S(2)}) async-start(), calls=%async_computation.7 | async-start | bytes 3932160 | tf_op jit(solution)/shard_map/reduce_scatter | solution.py:237
  377.5 183.9 %all-gather.11.cloned.1.call-start = ((), (), s32[]{:S(2)}) async-start(), calls=%async_computation.10 | async-start | bytes 3932160 | tf_op jit(solution)/shard_map/all_gather | solution.py:262
  497.8 235.9 %reduce-scatter.11.cloned.1.call-start = ((), (), s32[]{:S(2)}) async-start(), calls=%async_computation.11 | async-start | bytes 3932160 | tf_op jit(solution)/shard_map/reduce_scatter | solution.py:290
  571.0 2.9 copy-start.54
  571.0 2.9 copy-start.56
  577.1 3.0 copy-start.11
  599.8 3.0 copy-start.11
  622.6 3.0 copy-start.11
  645.4 3.0 copy-start.11
  667.2 3.5 copy-start.9
  668.0 3.7 copy-start.12
  674.5 179.0 %all-reduce.5.cloned.1.call-start = ((), (), s32[]{:S(2)}) async-start(), calls=%async_computation.12 | async-start | bytes 14155776 | tf_op jit(solution)/shard_map/psum | solution.py:317
  674.6 7.1 copy-start.48
  674.6 7.1 copy-start.58
  681.7 4.2 copy-start.25
  685.9 2.1 copy-start.16
  688.2 2.1 copy-start.2
  688.2 2.3 copy-start.10
  695.3 6.1 copy-start.15
  695.3 38.3 %copy-start.36 = (f32[768]{0:T(1024)S(1)}, f32[768]{0:T(1024)}, u32[]{:S(2)}) copy-start(f32[768]{0:T(1024)} %copy-done.35) | copy-start | bytes 9220
  695.4 38.3 %copy-start.38 = (f32[512]{0:T(512)S(1)}, f32[512]{0:T(512)}, u32[]{:S(2)}) copy-start(f32[512]{0:T(512)} %copy-done.37) | copy-start | bytes 6148
  695.4 38.3 %copy-start.41 = (f32[512]{0:T(512)S(1)}, f32[512]{0:T(512)}, u32[]{:S(2)}) copy-start(f32[512]{0:T(512)} %copy-done.40) | copy-start | bytes 6148
  700.0 35.7 %copy-start.44 = (f32[768]{0:T(1024)S(1)}, f32[768]{0:T(1024)}, u32[]{:S(2)}) copy-start(f32[768]{0:T(1024)} %get-tuple-element.258) | copy-start | bytes 9220
  733.6 43.9 %copy-start.18 = (bf16[512,768]{1,0:T(8,128)(2,1)S(1)}, bf16[512,768]{1,0:T(8,128)(2,1)}, u32[]{:S(2)}) copy-start(bf16[512,768]{1,0:T(8,128)(2,1)} %reduce-scatter.11.cloned.1.call-done) | copy-start | bytes 2359300
  853.5 2.1 copy-start.24
  853.5 2.9 copy-start.23
  853.5 3.7 copy-start.22
  855.6 2.5 copy-start.20
  858.0 2.5 copy-start.19
  (26 other events, 33.4 us)
Sparse Core Ops, SparseCore 0:
  12.4 66.1 all-gather.4
  163.9 58.8 reduce-scatter.4
  227.1 63.5 all-gather.6
  292.1 62.1 all-gather.8
  371.0 58.8 reduce-scatter.8
  432.1 60.2 reduce-scatter.6
  497.9 63.5 all-gather.10
  674.7 58.8 reduce-scatter.10
  738.8 114.6 all-reduce.4
where the time goes:
time: 874 us; the launch traced here: 869 us
  waiting for transfers between devices  492 us (56%)
  matrix products  186 us (21%)
  blocking collectives  67.4 us (8%)
  local copies, waits for them, and re-layouts  60 us (7%)
  other arithmetic  46.6 us (5%)
  between operations  14.6 us (2%)
    psum x1, waiting for transfers between devices, per_device(): lax.psum((query_weight_grad, query_bias_grad, key_weight_grad, value_weig...  73.2 us
    all_gather x1, waiting for transfers between devices, per_device(): first_rows = lax.all_gather(first_low, 'head', axis=0, tiled=True)  64 us
    all_gather x1, waiting for transfers between devices, per_device(): branch_rows = lax.all_gather(branch_low, 'head', axis=0, tiled=True)  63.6 us
    all_gather x1, waiting for transfers between devices, per_device(): second_rows = lax.all_gather(second_low, 'head', axis=0, tiled=True)  61.8 us
    reduce_scatter x1, waiting for transfers between devices, per_device(): lax.psum_scatter(jnp.dot(up_act, down_weight, preferred_element_type=jnp....  59 us
    reduce_scatter x1, waiting for transfers between devices, per_device(): lax.psum_scatter(jnp.dot(context, out_weight, preferred_element_type=jnp....  56.4 us
    all_gather x1, waiting for transfers between devices, per_device(): grad_rows = lax.all_gather(grad_output, 'head', axis=0, tiled=True)  56.1 us
    reduce_scatter x1, waiting for transfers between devices, per_device(): lax.psum_scatter(back_dot(grad_up, up_weight).astype(jnp.bfloat16), 'head...  51.2 us
  transfers between devices with their start and end apart: 9, of which 9 were waited for; matrix products, arithmetic and copies ran while one was open for 6% of the time, Pallas kernels for 0%

commit v1 on v0

--- a/solution.py
+++ b/solution.py
@@ -3,6 +3,16 @@
 import jax.numpy as jnp
 from jax import lax
 from jax.sharding import PartitionSpec as P
+
+
+def around_the_ring(block, mesh_axis, dim):
+    peers = lax.axis_size(mesh_axis)
+    held, blocks = (block, [block])
+    for _ in range(peers - 1):
+        held = lax.ppermute(held, mesh_axis, [(i, (i + 1) % peers) for i in range(peers)])
+        blocks.insert(0, held)
+    merged = jnp.concatenate(blocks, axis=dim)
+    return jnp.roll(merged, (lax.axis_index(mesh_axis) + 1) * block.shape[dim], axis=dim)
 
 
 def norm_stats(values_in):
@@ -186,7 +196,7 @@
     inputs = layer_input.astype(jnp.float32)
     normed_one, factor_one = norm_stats(inputs)
     first_low = (normed_one * first_gain + first_shift).astype(jnp.bfloat16)
-    first_rows = lax.all_gather(first_low, "head", axis=0, tiled=True)
+    first_rows = around_the_ring(first_low, "head", 0)
     total_rows = first_rows.shape[0]
     length = total_rows // segments
     queries = (

time: 874 us -> 871 us (level)
  waiting for transfers between devices: 492 us -> 482 us
    all_gather x1 -> x0, waiting for transfers between devices: 64 us -> none  [per_device(): first_rows = lax.all_gather(first_low, 'head', axis=0, tiled=True)]
    ppermute x0 -> x3, waiting for transfers between devices: none -> 54.4 us  [around_the_ring(): lax.ppermute(held, mesh_axis, [(i, (i + 1) % peers) for i in range(peers)])]
    unnamed x124 -> x134, local copies, waits for them, and re-layouts: 16.4 us -> 20.3 us
  transfers between devices with their start and end apart: 9 -> 11, of which waited for: 9 -> 11; matrix products, arithmetic and copies ran while one was open for 6% -> 7% of each run, Pallas kernels for 0% -> 0%
where the time goes in v1:
time: 871 us; the launch traced here: 864 us
  waiting for transfers between devices  482 us (55%)
  matrix products  183 us (21%)
  blocking collectives  67.1 us (8%)
  local copies, waits for them, and re-layouts  63.9 us (7%)
  other arithmetic  48 us (6%)
  between operations  15 us (2%)
    psum x1, waiting for transfers between devices, per_device(): lax.psum((query_weight_grad, query_bias_grad, key_weight_grad, value_weig...  73.1 us
    all_gather x1, waiting for transfers between devices, per_device(): branch_rows = lax.all_gather(branch_low, 'head', axis=0, tiled=True)  63.6 us
    all_gather x1, waiting for transfers between devices, per_device(): second_rows = lax.all_gather(second_low, 'head', axis=0, tiled=True)  61.4 us
    reduce_scatter x1, waiting for transfers between devices, per_device(): lax.psum_scatter(jnp.dot(up_act, down_weight, preferred_element_type=jnp....  59 us
    all_gather x1, waiting for transfers between devices, per_device(): grad_rows = lax.all_gather(grad_output, 'head', axis=0, tiled=True)  56.3 us
    reduce_scatter x1, waiting for transfers between devices, per_device(): lax.psum_scatter(jnp.dot(context, out_weight, preferred_element_type=jnp....  55.5 us
    ppermute x3, waiting for transfers between devices, around_the_ring(): lax.ppermute(held, mesh_axis, [(i, (i + 1) % peers) for i in range(peers)])  54.4 us
    reduce_scatter x1, waiting for transfers between devices, per_device(): lax.psum_scatter(back_dot(grad_up, up_weight).astype(jnp.bfloat16), 'head...  51.2 us
  transfers between devices with their start and end apart: 11, of which 11 were waited for; matrix products, arithmetic and copies ran while one was open for 7% of the time, Pallas kernels for 0%

profile of v1, /device:TPU:0, one launch (start us, length us, event | category | flops | bytes accessed | tf_op | source)
XLA Modules:
  0.0 864.3 jit_solution(3114026239799586349)
XLA Ops:
  10.7 3.1 collective-permute-start
  13.8 19.6 %collective-permute-done = bf16[512,768]{1,0:T(8,128)(2,1)S(1)} collective-permute-done((bf16[512,768]{1,0:T(8,128)(2,1)S(1)}, bf16[512,768]{1,0:T(8,128)(2,1)S(1)}, u32[]{:S(2)}, u32[]{:S(2)}) %collective-permute-start) | collective-permute-done | bytes 786464 | tf_op jit(solution)/shard_map/ppermute | solution.py:12
  33.4 20.6 %collective-permute-done.1 = bf16[512,768]{1,0:T(8,128)(2,1)} collective-permute-done((bf16[512,768]{1,0:T(8,128)(2,1)S(1)}, bf16[512,768]{1,0:T(8,128)(2,1)}, u32[]{:S(2)}, u32[]{:S(2)}) %collective-permute-start.1) | collective-permute-done | bytes 786464 | tf_op jit(solution)/shard_map/ppermute | solution.py:12
  57.3 2.4 fusion.205
  59.7 14.2 %collective-permute-done.2 = bf16[512,768]{1,0:T(8,128)(2,1)} collective-permute-done((bf16[512,768]{1,0:T(8,128)(2,1)}, bf16[512,768]{1,0:T(8,128)(2,1)}, u32[]{:S(2)}, u32[]{:S(2)}) %collective-permute-start.2) | collective-permute-done | bytes 786464 | tf_op jit(solution)/shard_map/ppermute | solution.py:12
  80.1 2.6 fusion.165
  82.6 2.0 convolution_convert_fusion.4
  88.6 3.2 reshape.257
  91.8 2.2 copy.58
  94.0 3.0 reshape.259
  96.9 2.2 copy.60
  100.1 54.4 %while.34 = (s32[]{:T(128)}, bf16[4,512,3,64]{1,3,2,0:T(8,128)(2,1)}, f32[4,3,512]{2,1,0:T(4,128)}, bf16[4,512,3,64]{1,3,2,0:T(8,128)(2,1)}, s32[4]{0:T(128)S(1)...) while((s32[]{:T(128)}, ...), condition=%wide.region_5.6_spmd, body=%wide.region_2.5_spmd.sunk | while | flops 325111296 | bytes 17297064 | solution.py:231
  110.5 3.2 fusion.335
  124.1 3.2 fusion.335
  135.1 2.0 fusion.332
  137.7 3.2 fusion.335
  151.3 3.2 fusion.335
  157.4 2.8 convolution_convert_fusion.2
  162.8 55.5 %reduce-scatter.5.cloned.1.call-done = bf16[512,768]{1,0:T(8,128)(2,1)} async-done(((bf16[2048,768]{1,0:T(8,128)(2,1)}), bf16[512,768]{1,0:T(8,128)(2,1)}) %reduce-scatter.5.cloned.1.call-update) | async-done | bytes 786448 | tf_op jit(solution)/shard_map/reduce_scatter | solution.py:235
  224.7 61.4 %all-gather.4.cloned.1.call-done = bf16[2048,768]{1,0:T(8,128)(2,1)} async-done(((bf16[512,768]{1,0:T(8,128)(2,1)}), bf16[2048,768]{1,0:T(8,128)(2,1)}) %all-gather.4.cloned.1.call-update) | async-done | bytes 3145744 | tf_op jit(solution)/shard_map/all_gather | solution.py:244
  286.1 7.5 fusion.217
  293.6 56.3 %all-gather.6.cloned.1.call-done = bf16[2048,768]{1,0:T(8,128)(2,1)} async-done(((bf16[512,768]{1,0:T(8,128)(2,1)}), bf16[2048,768]{1,0:T(8,128)(2,1)}) %all-gather.6.cloned.1.call-update) | async-done | bytes 3145744 | tf_op jit(solution)/shard_map/all_gather | solution.py:255
  349.9 11.0 %convert_reduce_fusion = (f32[768]{0:T(1024)}, bf16[2048,768]{1,0:T(8,128)(2,1)S(1)}, bf16[2048,768]{1,0:T(8,128)(2,1)}) fusion(f32[2048,768]{1,0:T(8,128)} %fusion.217, f32[768]{0:T(1024)} %convert_element_type.193, bf16[2048,768]{1,0:T(8,128)(2,1)} %all-gather.6.cloned.1.call-done, bf16[768,768]{1,0:T(8,128)(2,1)} %param.43), kind=kOutput, calls=%fused_computation.206 | convolution fusion | flops 2455239936 | bytes 16914432 | tf_op jit(solution)/shard_map/dot_general | solution.py:39
  362.5 4.0 convolution_convert_fusion
  366.7 6.5 convolution_convert_fusion.1
  374.5 51.2 %reduce-scatter.9.cloned.1.call-done = bf16[512,768]{1,0:T(8,128)(2,1)} async-done(((bf16[2048,768]{1,0:T(8,128)(2,1)}), bf16[512,768]{1,0:T(8,128)(2,1)}) %reduce-scatter.9.cloned.1.call-update) | async-done | bytes 786448 | tf_op jit(solution)/shard_map/reduce_scatter | solution.py:262
  425.7 2.9 fusion.188
  429.2 59.0 %reduce-scatter.7.cloned.1.call-done = bf16[512,768]{1,0:T(8,128)(2,1)} async-done(((bf16[2048,768]{1,0:T(8,128)(2,1)}), bf16[512,768]{1,0:T(8,128)(2,1)}) %reduce-scatter.7.cloned.1.call-update) | async-done | bytes 786448 | tf_op jit(solution)/shard_map/reduce_scatter | solution.py:247
  488.1 5.3 convert_reduce_fusion.5
  493.5 63.6 %all-gather.8.cloned.1.call-done = bf16[2048,768]{1,0:T(8,128)(2,1)} async-done(((bf16[512,768]{1,0:T(8,128)(2,1)}), bf16[2048,768]{1,0:T(8,128)(2,1)}) %all-gather.8.cloned.1.call-update) | async-done | bytes 3145744 | tf_op jit(solution)/shard_map/all_gather | solution.py:272
  557.1 4.0 convolution_convert_fusion.3
  561.1 3.4 reshape.263
  564.5 2.2 copy.64
  569.6 91.2 %while.35 = (s32[]{:T(128)}, bf16[4,512,3,64]{1,3,2,0:T(8,128)(2,1)}, bf16[4,512,3,64]{1,3,2,0:T(8,128)(2,1)}, bf16[4,512,3,64]{1,3,2,0:T(8,128)(2,1)}, bf16[4,2...) while((s32[]{:T(128)}, ...), condition=%wide.region_17.18_spmd, body=%wide.region_13.17_spmd.sunk | while | flops 795121152 | bytes 42630428 | solution.py:276
  575.7 2.7 fusion.362
  598.5 2.7 fusion.362
  621.2 2.7 fusion.362
  644.0 2.7 fusion.362
  667.1 2.8 add_convert_fusion.3
  669.9 7.1 fusion.222
  677.0 4.2 fusion.221
  696.5 25.3 %all-reduce.1 = (f32[192]{0:T(256)}, f32[192]{0:T(256)}, f32[768]{0:T(1024)}, f32[3,256]{1,0:T(4,128)}, f32[3,256]{1,0:T(4,128)}) all-reduce(f32[192]{0:T(256)} %reduce_sum.229, f32[192]{0:T(256)S(1)} %add.274, f32[768]{0:T(1024)} %get-tuple-element.347, f32[3,256]{1,0:T(4,128)} %reduce_sum.237, ...), channel_id=1, replica_groups=mesh['batch'=8,'head'=4] {'batch'}, use_global_device_ids=true, to_apply=%region_27.28 | all-reduce | flops 2688 | bytes 21504 | tf_op jit(solution)/shard_map/psum | solution.py:327
  721.8 7.1 reduce-scatter.11.cloned.1.call-done
  728.9 2.0 fusion.189
  731.0 41.8 %all-reduce = (f32[768]{0:T(1024)}, f32[768]{0:T(1024)}, f32[768]{0:T(1024)}, f32[768]{0:T(1024)}, f32[768]{0:T(1024)}, /*index=5*/f32[768]{0:T(1024)}) all-reduce(f32[768]{0:T(1024)S(1)} %get-tuple-element.260, f32[768]{0:T(1024)S(1)} %get-tuple-element.265, ...), channel_id=1, replica_groups=mesh['batch'=8,'head'=4] {'batch','head'}, use_global_device_ids=true, to_apply=%region_22.23 | all-reduce | flops 4608 | bytes 36864 | tf_op jit(solution)/shard_map/psum | solution.py:350
  772.8 2.9 fusion.182
  775.7 73.1 %all-reduce.5.cloned.1.call-done = (f32[768,192]{0,1:T(8,128)}, f32[768,192]{0,1:T(8,128)}, f32[768,192]{0,1:T(8,128)}, f32[192,768]{1,0:T(8,128)}, f32[768,768]{1,0:T(8,128)}, /*index=5*/f32[768,768]{1,0:T(8,128)}) async-done(((f32[768,192]{0,1:T(8,128)}, f32[768,192]{0,1:T(8,128)}, f32[768,192]{0,1:T(8,128)}, f32[192,768]{1,0:T(8,128)}, f32[768,768]{1,0:T(8,128)}, /*index=5*/f32[768,768]{1,0:T(8,128)}), ...) | async-done | bytes 7077904 | tf_op jit(solution)/shard_map/psum | solution.py:327
  848.8 2.0 copy.229
  (381 shorter events, 182.9 us)
Async XLA Ops:
  7.2 48.5 %copy-start = (bf16[4,256,768]{2,1,0:T(8,128)(2,1)S(1)}, bf16[4,256,768]{2,1,0:T(8,128)(2,1)}, u32[]{:S(2)}) copy-start(bf16[4,256,768]{2,1,0:T(8,128)(2,1)} %param.29) | copy-start | bytes 4718596
  7.2 3.2 copy-start.1
  7.2 3.1 copy-start.43
  7.2 3.1 copy-start.44
  7.2 46.8 %copy-start.48 = (s32[4]{0:T(128)S(1)}, s32[4]{0:T(128)}, u32[]{:S(2)}) copy-start(s32[4]{0:T(128)} %param.27) | copy-start | bytes 52
  7.2 47.3 %copy-start.49 = (bf16[192]{0:T(256)(128)(2,1)S(1)}, bf16[192]{0:T(256)(128)(2,1)}, u32[]{:S(2)}) copy-start(bf16[192]{0:T(256)(128)(2,1)} %param.36) | copy-start | bytes 1156
  7.3 47.8 %copy-start.50 = (bf16[192]{0:T(256)(128)(2,1)S(1)}, bf16[192]{0:T(256)(128)(2,1)}, u32[]{:S(2)}) copy-start(bf16[192]{0:T(256)(128)(2,1)} %param.33) | copy-start | bytes 1156
  7.3 211.1 %reduce-scatter.5.cloned.1.call-start = ((), (), s32[]{:S(2)}) async-start(), calls=%async_computation.4 | async-start | bytes 3932160 | tf_op jit(solution)/shard_map/reduce_scatter | solution.py:235
  8.8 70.4 %copy-start.35 = (f32[512]{0:T(512)}, f32[512]{0:T(512)S(1)}, u32[]{:S(2)}) copy-start(f32[512]{0:T(512)S(1)} %broadcast_multiply_fusion.7) | copy-start | bytes 6148
  10.3 68.9 %copy-start.37 = (f32[512]{0:T(512)}, f32[512]{0:T(512)S(1)}, u32[]{:S(2)}) copy-start(f32[512]{0:T(512)S(1)} %add_rsqrt_fusion.1) | copy-start | bytes 6148
  10.3 68.9 %copy-start.33 = (f32[768]{0:T(1024)}, f32[768]{0:T(1024)S(1)}, u32[]{:S(2)}) copy-start(f32[768]{0:T(1024)S(1)} %convert_element_type.176) | copy-start | bytes 9220
  10.7 22.6 %collective-permute-start = (bf16[512,768]{1,0:T(8,128)(2,1)S(1)}, bf16[512,768]{1,0:T(8,128)(2,1)S(1)}, u32[]{:S(2)}, u32[]{:S(2)}) collective-permute-start(bf16[512,768]{1,0:T(8,128)(2,1)S(1)} %fusion.178), channel_id=1, source_target_pairs={{0,1},{1,2},{2,3},{3,0},{4,5},{5,6},{6,7},{7,4},{8,9},{9,10},{10,1... | collective-permute-start | bytes 2359304 | tf_op jit(solution)/shard_map/ppermute | solution.py:12
  33.4 20.6 %collective-permute-start.1 = (bf16[512,768]{1,0:T(8,128)(2,1)S(1)}, bf16[512,768]{1,0:T(8,128)(2,1)}, u32[]{:S(2)}, u32[]{:S(2)}) collective-permute-start(bf16[512,768]{1,0:T(8,128)(2,1)S(1)} %collective-permute-done), channel_id=1, source_target_pairs={{0,1},{1,2},{2,3},{3,0},{4,5},{5,6},{6,7},{7,4},{8,9},{9,10},{10,1... | collective-permute-start | bytes 2359304 | tf_op jit(solution)/shard_map/ppermute | solution.py:12
  54.0 19.9 %collective-permute-start.2 = (bf16[512,768]{1,0:T(8,128)(2,1)}, bf16[512,768]{1,0:T(8,128)(2,1)}, u32[]{:S(2)}, u32[]{:S(2)}) collective-permute-start(bf16[512,768]{1,0:T(8,128)(2,1)} %collective-permute-done.1), channel_id=1, source_target_pairs={{0,1},{1,2},{2,3},{3,0},{4,5},{5,6},{6,7},{7,4},{8,9},{9,10},{10,1... | collective-permute-start | bytes 2359304 | tf_op jit(solution)/shard_map/ppermute | solution.py:12
  80.1 4.6 copy-start.4
  96.9 3.2 copy-start.31
  96.9 3.2 copy-start.32
  96.9 3.2 copy-start.51
  96.9 3.2 copy-start.55
  154.5 2.9 copy-start.28
  160.2 125.9 %all-gather.4.cloned.1.call-start = ((), (), s32[]{:S(2)}) async-start(), calls=%async_computation.5 | async-start | bytes 3932160 | tf_op jit(solution)/shard_map/all_gather | solution.py:244
  222.4 127.4 %all-gather.6.cloned.1.call-start = ((), (), s32[]{:S(2)}) async-start(), calls=%async_computation.7 | async-start | bytes 3932160 | tf_op jit(solution)/shard_map/all_gather | solution.py:255
  223.2 202.5 %reduce-scatter.9.cloned.1.call-start = ((), (), s32[]{:S(2)}) async-start(), calls=%async_computation.8 | async-start | bytes 3932160 | tf_op jit(solution)/shard_map/reduce_scatter | solution.py:262
  349.9 12.7 %copy-start.47 = (bf16[768,768]{1,0:T(8,128)(2,1)S(1)}, bf16[768,768]{1,0:T(8,128)(2,1)}, u32[]{:S(2)}) copy-start(bf16[768,768]{1,0:T(8,128)(2,1)} %param.41) | copy-start | bytes 3538948
  366.6 121.5 %reduce-scatter.7.cloned.1.call-start = ((), (), s32[]{:S(2)}) async-start(), calls=%async_computation.6 | async-start | bytes 3932160 | tf_op jit(solution)/shard_map/reduce_scatter | solution.py:247
  373.2 183.9 %all-gather.8.cloned.1.call-start = ((), (), s32[]{:S(2)}) async-start(), calls=%async_computation.9 | async-start | bytes 3932160 | tf_op jit(solution)/shard_map/all_gather | solution.py:272
  493.4 235.5 %reduce-scatter.11.cloned.1.call-start = ((), (), s32[]{:S(2)}) async-start(), calls=%async_computation.10 | async-start | bytes 3932160 | tf_op jit(solution)/shard_map/reduce_scatter | solution.py:300
  566.7 2.9 copy-start.52
  566.7 2.9 copy-start.56
  572.7 3.0 copy-start.9
  595.5 3.0 copy-start.9
  618.2 3.0 copy-start.9
  641.0 3.0 copy-start.9
  663.6 3.4 copy-start.10
  669.9 178.9 %all-reduce.5.cloned.1.call-start = ((), (), s32[]{:S(2)}) async-start(), calls=%async_computation.11 | async-start | bytes 14155776 | tf_op jit(solution)/shard_map/psum | solution.py:327
  669.9 7.1 copy-start.46
  669.9 7.1 copy-start.58
  669.9 12.7 %slice-start = ((s8[6291456]{0:T(1024)(128)(4,1)}), s8[4194304]{0:T(1024)(128)(4,1)S(1)}, s32[]{:S(2)}) async-start(s8[6291456]{0:T(1024)(128)(4,1)} %bitcast.373), calls=%async_computation.12 | async-start | bytes 8388608
  677.0 4.2 copy-start.23
  677.0 5.7 slice-start.1
  690.1 6.1 copy-start.13
  690.1 38.8 %copy-start.34 = (f32[768]{0:T(1024)S(1)}, f32[768]{0:T(1024)}, u32[]{:S(2)}) copy-start(f32[768]{0:T(1024)} %copy-done.33) | copy-start | bytes 9220
  690.1 38.8 %copy-start.36 = (f32[512]{0:T(512)S(1)}, f32[512]{0:T(512)}, u32[]{:S(2)}) copy-start(f32[512]{0:T(512)} %copy-done.35) | copy-start | bytes 6148
  690.1 38.8 %copy-start.38 = (f32[512]{0:T(512)S(1)}, f32[512]{0:T(512)}, u32[]{:S(2)}) copy-start(f32[512]{0:T(512)} %copy-done.37) | copy-start | bytes 6148
  694.7 36.2 %copy-start.42 = (f32[768]{0:T(1024)S(1)}, f32[768]{0:T(1024)}, u32[]{:S(2)}) copy-start(f32[768]{0:T(1024)} %get-tuple-element.258) | copy-start | bytes 9220
  728.9 43.9 %copy-start.16 = (bf16[512,768]{1,0:T(8,128)(2,1)S(1)}, bf16[512,768]{1,0:T(8,128)(2,1)}, u32[]{:S(2)}) copy-start(bf16[512,768]{1,0:T(8,128)(2,1)} %reduce-scatter.11.cloned.1.call-done) | copy-start | bytes 2359300
  848.8 2.9 copy-start.21
  848.8 3.7 copy-start.20
  (30 other events, 47.5 us)
Sparse Core Ops, SparseCore 0:
  160.3 57.9 reduce-scatter.4
  222.5 63.5 all-gather.3
  287.7 62.1 all-gather.5
  366.7 58.8 reduce-scatter.8
  427.8 60.2 reduce-scatter.6
  493.6 63.5 all-gather.7
  670.0 58.8 reduce-scatter.10
  734.1 114.6 all-reduce.4
